TPU v7x, 32 devices: a whole 2x2x4 slice. The times are simulated.
32 devices in a mesh: dp: 8 (over z, y), tensor: 4 (over x, core).
Axes of the slice: x: 2, y: 2, z: 4, core: 2. Of those that a mesh axis runs over, the one named last changes fastest.
Arguments:
- gradients: bfloat16 [8, 2, 256, 1792], P('dp', None, None, 'tensor'), may hold values from -16 to 16, as said below
- errors: float32 [8, 2, 256, 1792], P('dp', None, None, 'tensor'), may hold values from -4 to 4
- start_factors: float32 [2, 1792, 32], P(None, 'tensor'), may hold values from -5 to 5
- moments: float32 [2, 256, 1792], P(None, 'dp', 'tensor'), may hold values from -2 to 2
- weights: float32 [2, 256, 1792], P(None, 'dp', 'tensor'), may hold values from -5 to 5
- vector_grads: bfloat16 [8, 5, 1792], P('dp', None, 'tensor'), may hold values from -16 to 16, as said below
- vector_moments: float32 [5, 1792], P(None, 'tensor'), may hold values from -2 to 2
- vector_weights: float32 [5, 1792], P(None, 'tensor'), may hold values from 0.5 to 1.5
Outputs:
- new_errors: float32 [8, 2, 256, 1792], P('dp', None, None, 'tensor')
- new_moments: float32 [2, 256, 1792], P(None, 'dp', 'tensor')
- new_weights: bfloat16 [2, 256, 1792], P(None, None, 'tensor')
- new_vector_moments: float32 [5, 1792], P(None, 'tensor')
- new_vector_weights: float32 [5, 1792], P(None, 'tensor')
Inputs may be any that keep to these rules, and one draw needn't show every extreme that they name: `gradients`: each replica's gradient is a part common to all replicas plus its own part. `vector_grads`: each replica's gradient is a part common to all replicas plus its own part.
All inputs are finite; a program needn't handle non-finite values.
Results may differ from a plain program's by a relative error of at most 0.0004.
Values may be sent and summed in bfloat16 or wider, within the bound.
A program may use at most 64 MiB of HBM per device.

v0:
```python
import jax
import jax.numpy as jnp
from jax import lax
from jax.sharding import PartitionSpec as P

ROUNDS = 2
momentum_coef = 0.9
step_rate = 0.1


def basis_from(gram_mat, summed):
    factor_low = jnp.linalg.cholesky(gram_mat)
    return lax.linalg.triangular_solve(
        factor_low, summed, left_side=False, lower=True, transpose_a=True
    )


def left_basis(mixed, right_f):
    partial_value = jnp.einsum("mkd,mdr->mkr", mixed, right_f, precision=lax.Precision.HIGHEST)
    summed = lax.psum(partial_value, ("dp", "tensor"))
    gram_mat = jnp.einsum("mkr,mks->mrs", summed, summed, precision=lax.Precision.HIGHEST)
    return basis_from(gram_mat, summed)


def update(mixed, start, moments, weights):
    right_f = start
    for round_idx in range(ROUNDS):
        basis_now = left_basis(mixed, right_f)
        right_part = jnp.einsum("mkd,mkr->mdr", mixed, basis_now, precision=lax.Precision.HIGHEST)
        right_f = lax.psum(right_part, "dp")
    replicas = lax.axis_size("dp")
    approx = (
        jnp.einsum("mkr,mdr->mkd", basis_now, right_f, precision=lax.Precision.HIGHEST) / replicas
    )
    fresh_errors = mixed - approx
    own_rows = moments.shape[1]
    my_rows = lax.dynamic_slice_in_dim(approx, lax.axis_index("dp") * own_rows, own_rows, 1)
    fresh_moments = momentum_coef * moments + my_rows
    fresh_weights = (weights - step_rate * fresh_moments).astype(jnp.bfloat16)
    regathered = lax.all_gather(fresh_weights, "dp", axis=1, tiled=True)
    return (fresh_errors, fresh_moments, regathered)


def per_device(
    gradients, errors, start_factors, moments, weights, vector_grads, vector_moments, vector_weights
):
    mixed = gradients[0].astype(jnp.float32) + errors[0]
    fresh_errors, fresh_moments, regathered = update(mixed, start_factors, moments, weights)
    vector_total = lax.psum(vector_grads[0].astype(jnp.float32), "dp")
    vector_mean = vector_total / lax.axis_size("dp")
    fresh_vector_moments = momentum_coef * vector_moments + vector_mean
    fresh_vector_weights = vector_weights - step_rate * fresh_vector_moments
    return (
        fresh_errors[None],
        fresh_moments,
        regathered,
        fresh_vector_moments,
        fresh_vector_weights,
    )


def solution(mesh):
    in_specs = (
        P("dp", None, None, "tensor"),
        P("dp", None, None, "tensor"),
        P(None, "tensor", None),
        P(None, "dp", "tensor"),
        P(None, "dp", "tensor"),
        P("dp", None, "tensor"),
        P(None, "tensor"),
        P(None, "tensor"),
    )
    out_specs = (
        P("dp", None, None, "tensor"),
        P(None, "dp", "tensor"),
        P(None, None, "tensor"),
        P(None, "tensor"),
        P(None, "tensor"),
    )
    return jax.shard_map(
        per_device, mesh=mesh, in_specs=in_specs, out_specs=out_specs, check_vma=False
    )
```

profile of v0, /device:TPU:0, one launch (start us, length us, event | category | flops | bytes accessed | tf_op | source)
XLA Modules:
  0.0 471.9 jit_solution(15930844537223940268)
XLA Ops:
  7.2 0.8 copy-done
  8.1 2.6 fusion.6
  10.8 123.7 %all-reduce.5.cloned.1.call-done = f32[2,256,32]{1,2,0:T(8,128)} async-done(((f32[2,256,32]{1,2,0:T(8,128)}), f32[2,256,32]{1,2,0:T(8,128)}) %all-reduce.5.cloned.1.call-update) | async-done | bytes 65552 | tf_op jit(solution)/shard_map/psum | solution.py:20
  134.5 1.1 fusion.13
  135.7 5.9 %custom-call.8 = f32[2,32,32]{2,1,0:T(8,128)S(1)} custom-call(f32[2,32,32]{2,1,0:T(8,128)S(1)} %fusion.12), custom_call_target="Cholesky" | custom-call | tf_op jit(solution)/shard_map/jit(cholesky)/cholesky | solution.py:12
  141.8 4.9 %custom-call.9 = f32[2,1,32,32]{2,3,1,0:T(8,128)S(1)} custom-call(f32[2,1,32,32]{3,2,1,0:T(8,128)S(1)} %select_bitcast_fusion.1), custom_call_target="InvertDiagBlocksLowerTriangular" | custom-call | tf_op jit(solution)/shard_map/triangular_solve/custom-call.0 | solution.py:13
  146.7 1.1 convolution_bitcast_fusion.1
  147.8 1.6 fusion.4
  149.5 70.5 %all-reduce.7.cloned.1.call-done = f32[2,448,32]{1,2,0:T(8,128)} async-done(((f32[2,448,32]{1,2,0:T(8,128)}), f32[2,448,32]{1,2,0:T(8,128)}) %all-reduce.7.cloned.1.call-update) | async-done | bytes 114704 | tf_op jit(solution)/shard_map/psum | solution.py:30
  220.0 2.3 fusion.2
  223.2 0.7 copy-done.5
  224.1 35.5 %psum.39 = f32[5,448]{1,0:T(8,128)S(1)} all-reduce(f32[5,448]{1,0:T(8,128)S(1)} %bitcast_convert_fusion), channel_id=1, replica_groups=mesh['dp'=8,'tensor'=4] {'dp'}, use_global_device_ids=true, to_apply=%region_6.9 | all-reduce | flops 2240 | bytes 17920 | tf_op jit(solution)/shard_map/psum | solution.py:49
  259.6 84.4 %all-reduce.9.cloned.1.call-done = f32[2,256,32]{1,2,0:T(8,128)} async-done(((f32[2,256,32]{1,2,0:T(8,128)}), f32[2,256,32]{1,2,0:T(8,128)}) %all-reduce.9.cloned.1.call-update) | async-done | bytes 65552 | tf_op jit(solution)/shard_map/psum | solution.py:20
  344.0 1.1 fusion.14
  345.2 5.9 %custom-call.10 = f32[2,32,32]{2,1,0:T(8,128)S(1)} custom-call(f32[2,32,32]{2,1,0:T(8,128)S(1)} %fusion.10), custom_call_target="Cholesky" | custom-call | tf_op jit(solution)/shard_map/jit(cholesky)/cholesky | solution.py:12
  351.3 4.9 %custom-call.11 = f32[2,1,32,32]{2,3,1,0:T(8,128)S(1)} custom-call(f32[2,1,32,32]{3,2,1,0:T(8,128)S(1)} %select_bitcast_fusion), custom_call_target="InvertDiagBlocksLowerTriangular" | custom-call | tf_op jit(solution)/shard_map/triangular_solve/custom-call.0 | solution.py:13
  356.5 1.6 fusion
  358.1 0.7 copy-done.6
  359.4 69.2 %all-reduce.11.cloned.1.call-done = f32[2,448,32]{1,2,0:T(8,128)} async-done(((f32[2,448,32]{1,2,0:T(8,128)}), f32[2,448,32]{1,2,0:T(8,128)}) %all-reduce.11.cloned.1.call-update) | async-done | bytes 114704 | tf_op jit(solution)/shard_map/psum | solution.py:30
  428.7 1.8 convolution_multiply_fusion
  430.5 1.1 fusion.8
  431.9 0.8 copy.34
  432.8 31.5 %all_gather.3 = bf16[2,256,448]{2,0,1:T(2,128)(2,1)S(1)} all-gather(bf16[2,32,448]{2,0,1:T(2,128)(2,1)S(1)} %copy.33), channel_id=1, replica_groups=mesh['dp'=8,'tensor'=4] {'dp'}, dimensions={1}, use_global_device_ids=true | all-gather | bytes 516096 | tf_op jit(solution)/shard_map/all_gather | solution.py:40
  464.3 1.1 copy.35
  (42 shorter events, 3.1 us)
Async XLA Ops:
  7.2 0.9 copy-start
  7.2 140.6 %copy-start.1 = (f32[1,2,256,448]{2,3,1,0:T(8,128)S(1)}, f32[1,2,256,448]{2,3,1,0:T(8,128)}, u32[]{:S(2)}) copy-start(f32[1,2,256,448]{2,3,1,0:T(8,128)} %param.12) | copy-start | bytes 2752516
  7.2 127.3 %all-reduce.5.cloned.1.call-start = ((), (), s32[]{:S(2)}) async-start(), calls=%async_computation | async-start | bytes 131072 | tf_op jit(solution)/shard_map/psum | solution.py:20
  10.7 137.1 %copy-start.2 = (bf16[1,2,256,448]{2,3,1,0:T(8,128)(2,1)S(1)}, bf16[1,2,256,448]{2,3,1,0:T(8,128)(2,1)}, u32[]{:S(2)}) copy-start(bf16[1,2,256,448]{2,3,1,0:T(8,128)(2,1)} %param.11) | copy-start | bytes 1376260
  10.7 209.3 %all-reduce.7.cloned.1.call-start = ((), (), s32[]{:S(2)}) async-start(), calls=%async_computation.1 | async-start | bytes 262144 | tf_op jit(solution)/shard_map/psum | solution.py:30
  149.5 194.5 %all-reduce.9.cloned.1.call-start = ((), (), s32[]{:S(2)}) async-start(), calls=%async_computation.2 | async-start | bytes 131072 | tf_op jit(solution)/shard_map/psum | solution.py:20
  220.0 3.0 copy-start.4
  222.3 0.7 copy-start.8
  222.3 206.3 %all-reduce.11.cloned.1.call-start = ((), (), s32[]{:S(2)}) async-start(), calls=%async_computation.3 | async-start | bytes 262144 | tf_op jit(solution)/shard_map/psum | solution.py:30
  223.0 0.9 copy-start.5
  345.1 11.0 %copy-start.3 = (f32[2,256,32]{1,2,0:T(8,128)S(1)}, f32[2,256,32]{1,2,0:T(8,128)}, u32[]{:S(2)}) copy-start(f32[2,256,32]{1,2,0:T(8,128)} %all-reduce.9.cloned.1.call-done) | copy-start | bytes 196612
  358.1 0.7 copy-start.6
  358.1 0.7 copy-start.7
Sparse Core Ops, SparseCore 0:
  14.2 120.2 all-reduce.4
  149.6 70.3 all-reduce.6
  227.1 116.7 all-reduce.8
  358.2 70.3 all-reduce.10
where the time goes:
time: 472 us
  waiting for transfers between devices  348 us (74%)
  blocking collectives  67 us (14%)
  other arithmetic  23.9 us (5%)
  between operations  13.9 us (3%)
  matrix products  13.6 us (3%)
  local copies, waits for them, and re-layouts  5.47 us (1%)
    psum x2, waiting for transfers between devices, left_basis(): summed = lax.psum(partial_value, ('dp', 'tensor'))  208 us
    psum x2, waiting for transfers between devices, update(): right_f = lax.psum(right_part, 'dp')  140 us
    psum x1, blocking collectives, per_device(): vector_total = lax.psum(vector_grads[0].astype(jnp.float32), 'dp')  35.5 us
    all_gather x1, blocking collectives, update(): regathered = lax.all_gather(fresh_weights, 'dp', axis=1, tiled=True)  31.5 us
    another operation x7, other arithmetic, basis_from(): factor_low = jnp.linalg.cholesky(gram_mat)  12 us
    another operation x5, other arithmetic, basis_from(): lax.linalg.triangular_solve(factor_low, summed, left_side=False, lower=Tr...  9.99 us
  transfers between devices with their start and end apart: 4, of which 4 were waited for; matrix products, arithmetic and copies ran while one was open for 0% of the time, Pallas kernels for 0%

commit v1 on v0

--- a/solution.py
+++ b/solution.py
@@ -37,7 +37,21 @@
     my_rows = lax.dynamic_slice_in_dim(approx, lax.axis_index("dp") * own_rows, own_rows, 1)
     fresh_moments = momentum_coef * moments + my_rows
     fresh_weights = (weights - step_rate * fresh_moments).astype(jnp.bfloat16)
-    regathered = lax.all_gather(fresh_weights, "dp", axis=1, tiled=True)
+    ways, here, turn = (lax.axis_size("dp"), lax.axis_index("dp"), fresh_weights.shape[1])
+    shape = [n * ways if d == 1 else n for d, n in enumerate(fresh_weights.shape)]
+    full = lax.dynamic_update_slice_in_dim(
+        jnp.zeros(shape, fresh_weights.dtype), fresh_weights, here * turn, axis=1
+    )
+    going_up = going_down = fresh_weights
+    for far in range(1, ways // 2 + 1):
+        going_up = lax.ppermute(going_up, "dp", [(d, (d + 1) % ways) for d in range(ways)])
+        full = lax.dynamic_update_slice_in_dim(full, going_up, (here - far) % ways * turn, axis=1)
+        if 2 * far < ways:
+            going_down = lax.ppermute(going_down, "dp", [(d, (d - 1) % ways) for d in range(ways)])
+            full = lax.dynamic_update_slice_in_dim(
+                full, going_down, (here + far) % ways * turn, axis=1
+            )
+    regathered = full
     return (fresh_errors, fresh_moments, regathered)
 
 

time: 472 us -> 518 us (1.097)
  waiting for transfers between devices: 348 us -> 396 us
  blocking collectives: 67 us -> 35.3 us
  local copies, waits for them, and re-layouts: 5.47 us -> 22 us
  starting transfers between devices: 0.16 us -> 11.5 us
    psum x2, waiting for transfers between devices: 208 us -> 245 us  [left_basis(): summed = lax.psum(partial_value, ('dp', 'tensor'))]
    all_gather x1 -> x0, blocking collectives: 31.5 us -> none  [update(): regathered = lax.all_gather(fresh_weights, 'dp', axis=1, tiled=True)]
    dynamic_update_slice x0 -> x8, local copies, waits for them, and re-layouts: none -> 16.6 us  [the longest x4 7.88 us: update(): lax.dynamic_update_slice_in_dim(full, going_up, (here - far) % ways * tur...]
    ppermute x0 -> x7, waiting for transfers between devices: none -> 12.6 us  [the longest x3 6.92 us: update(): lax.ppermute(going_down, 'dp', [(d, (d - 1) % ways) for d in range(ways)])]
    ppermute x0 -> x7, starting transfers between devices: none -> 11.3 us  [the longest x4 7.34 us: update(): lax.ppermute(going_up, 'dp', [(d, (d + 1) % ways) for d in range(ways)])]
  transfers between devices with their start and end apart: 4 -> 11, of which waited for: 4 -> 6; matrix products, arithmetic and copies ran while one was open for 0% -> 4% of each run, Pallas kernels for 0% -> 0%
where the time goes in v1:
time: 518 us; the launch traced here: 517 us
  waiting for transfers between devices  396 us (76%)
  blocking collectives  35.3 us (7%)
  other arithmetic  24.6 us (5%)
  local copies, waits for them, and re-layouts  22 us (4%)
  between operations  14 us (3%)
  matrix products  13.6 us (3%)
  starting transfers between devices  11.5 us (2%)
    psum x2, waiting for transfers between devices, left_basis(): summed = lax.psum(partial_value, ('dp', 'tensor'))  245 us
    psum x2, waiting for transfers between devices, update(): right_f = lax.psum(right_part, 'dp')  138 us
    psum x1, blocking collectives, per_device(): vector_total = lax.psum(vector_grads[0].astype(jnp.float32), 'dp')  35.3 us
    another operation x7, other arithmetic, basis_from(): factor_low = jnp.linalg.cholesky(gram_mat)  12 us
  transfers between devices with their start and end apart: 11, of which 6 were waited for; matrix products, arithmetic and copies ran while one was open for 4% of the time, Pallas kernels for 0%

profile of v1, /device:TPU:0, one launch (start us, length us, event | category | flops | bytes accessed | tf_op | source)
XLA Modules:
  0.0 517.3 jit_solution(17698577803345100730)
XLA Ops:
  8.1 2.6 fusion.6
  10.8 123.6 %all-reduce.5.cloned.1.call-done = f32[2,256,32]{1,2,0:T(8,128)} async-done(((f32[2,256,32]{1,2,0:T(8,128)}), f32[2,256,32]{1,2,0:T(8,128)}) %all-reduce.5.cloned.1.call-update) | async-done | bytes 65552 | tf_op jit(solution)/shard_map/psum | solution.py:20
  135.7 5.9 %custom-call.8 = f32[2,32,32]{2,1,0:T(8,128)S(1)} custom-call(f32[2,32,32]{2,1,0:T(8,128)S(1)} %fusion.12), custom_call_target="Cholesky" | custom-call | tf_op jit(solution)/shard_map/jit(cholesky)/cholesky | solution.py:12
  141.7 4.9 custom-call.9
  149.5 70.5 %all-reduce.7.cloned.1.call-done = f32[2,448,32]{1,2,0:T(8,128)} async-done(((f32[2,448,32]{1,2,0:T(8,128)}), f32[2,448,32]{1,2,0:T(8,128)}) %all-reduce.7.cloned.1.call-update) | async-done | bytes 114704 | tf_op jit(solution)/shard_map/psum | solution.py:30
  220.0 2.2 fusion.2
  222.3 121.6 %all-reduce.9.cloned.1.call-done = f32[2,256,32]{1,2,0:T(8,128)} async-done(((f32[2,256,32]{1,2,0:T(8,128)}), f32[2,256,32]{1,2,0:T(8,128)}) %all-reduce.9.cloned.1.call-update) | async-done | bytes 65552 | tf_op jit(solution)/shard_map/psum | solution.py:20
  345.2 5.9 %custom-call.10 = f32[2,32,32]{2,1,0:T(8,128)S(1)} custom-call(f32[2,32,32]{2,1,0:T(8,128)S(1)} %fusion.10), custom_call_target="Cholesky" | custom-call | tf_op jit(solution)/shard_map/jit(cholesky)/cholesky | solution.py:12
  351.3 4.9 custom-call.11
  360.9 67.8 %all-reduce.11.cloned.1.call-done = f32[2,448,32]{1,2,0:T(8,128)} async-done(((f32[2,448,32]{1,2,0:T(8,128)}), f32[2,448,32]{1,2,0:T(8,128)}) %all-reduce.11.cloned.1.call-update) | async-done | bytes 114704 | tf_op jit(solution)/shard_map/psum | solution.py:30
  428.7 1.9 convolution_multiply_fusion
  432.3 3.9 collective-permute-start.1
  436.2 5.7 %collective-permute-done = bf16[2,32,448]{1,2,0:T(8,128)(2,1)S(1)} collective-permute-done((bf16[2,32,448]{1,2,0:T(8,128)(2,1)}, bf16[2,32,448]{1,2,0:T(8,128)(2,1)S(1)}, u32[]{:S(2)}, u32[]{:S(2)}) %collective-permute-start) | collective-permute-done | bytes 57376 | tf_op jit(solution)/shard_map/ppermute | solution.py:47
  441.9 2.5 collective-permute-start.2
  444.4 35.3 %psum.39 = f32[5,448]{1,0:T(8,128)S(1)} all-reduce(f32[5,448]{1,0:T(8,128)S(1)} %bitcast_convert_fusion), channel_id=1, replica_groups=mesh['dp'=8,'tensor'=4] {'dp'}, use_global_device_ids=true, to_apply=%region_6.9 | all-reduce | flops 2240 | bytes 17920 | tf_op jit(solution)/shard_map/psum | solution.py:63
  479.7 2.0 collective-permute-start.4
  482.4 6.9 %collective-permute-done.3 = bf16[2,32,448]{1,2,0:T(8,128)(2,1)} collective-permute-done((bf16[2,32,448]{1,2,0:T(8,128)(2,1)S(1)}, bf16[2,32,448]{1,2,0:T(8,128)(2,1)}, u32[]{:S(2)}, u32[]{:S(2)}) %collective-permute-start.3) | collective-permute-done | bytes 57376 | tf_op jit(solution)/shard_map/ppermute | solution.py:50
  489.3 2.0 collective-permute-start.6
  492.4 1.8 dynamic_update_slice.24
  496.6 1.9 dynamic_update_slice.26
  498.5 2.4 dynamic_update_slice.27
  500.9 2.5 dynamic_update_slice.28
  503.4 2.4 dynamic_update_slice.29
  505.8 2.5 dynamic_update_slice.30
  (66 shorter events, 19.5 us)
Async XLA Ops:
  7.2 0.9 copy-start
  7.2 140.6 %copy-start.1 = (f32[1,2,256,448]{2,3,1,0:T(8,128)S(1)}, f32[1,2,256,448]{2,3,1,0:T(8,128)}, u32[]{:S(2)}) copy-start(f32[1,2,256,448]{2,3,1,0:T(8,128)} %param.12) | copy-start | bytes 2752516
  7.2 127.3 %all-reduce.5.cloned.1.call-start = ((), (), s32[]{:S(2)}) async-start(), calls=%async_computation | async-start | bytes 131072 | tf_op jit(solution)/shard_map/psum | solution.py:20
  10.7 137.1 %copy-start.2 = (bf16[1,2,256,448]{2,3,1,0:T(8,128)(2,1)S(1)}, bf16[1,2,256,448]{2,3,1,0:T(8,128)(2,1)}, u32[]{:S(2)}) copy-start(bf16[1,2,256,448]{2,3,1,0:T(8,128)(2,1)} %param.11) | copy-start | bytes 1376260
  10.7 209.3 %all-reduce.7.cloned.1.call-start = ((), (), s32[]{:S(2)}) async-start(), calls=%async_computation.1 | async-start | bytes 262144 | tf_op jit(solution)/shard_map/psum | solution.py:30
  149.5 194.5 %all-reduce.9.cloned.1.call-start = ((), (), s32[]{:S(2)}) async-start(), calls=%async_computation.2 | async-start | bytes 131072 | tf_op jit(solution)/shard_map/psum | solution.py:20
  222.3 206.4 %all-reduce.11.cloned.1.call-start = ((), (), s32[]{:S(2)}) async-start(), calls=%async_computation.3 | async-start | bytes 262144 | tf_op jit(solution)/shard_map/psum | solution.py:30
  345.2 11.0 %copy-start.4 = (f32[2,256,32]{1,2,0:T(8,128)S(1)}, f32[2,256,32]{1,2,0:T(8,128)}, u32[]{:S(2)}) copy-start(f32[2,256,32]{1,2,0:T(8,128)} %all-reduce.9.cloned.1.call-done) | copy-start | bytes 196612
  358.1 0.9 copy-start.6
  359.0 0.9 copy-start.7
  428.7 1.9 copy-start.3
  430.6 13.8 %copy-start.10 = (bf16[1,5,448]{2,1,0:T(8,128)(2,1)S(1)}, bf16[1,5,448]{2,1,0:T(8,128)(2,1)}, u32[]{:S(2)}) copy-start(bf16[1,5,448]{2,1,0:T(8,128)(2,1)} %param.16) | copy-start | bytes 13444
  431.5 10.4 %collective-permute-start = (bf16[2,32,448]{1,2,0:T(8,128)(2,1)}, bf16[2,32,448]{1,2,0:T(8,128)(2,1)S(1)}, u32[]{:S(2)}, u32[]{:S(2)}) collective-permute-start(bf16[2,32,448]{1,2,0:T(8,128)(2,1)} %get-tuple-element.19), channel_id=1, source_target_pairs={{0,4},{4,8},{8,12},{12,16},{16,20},{20,24},{24,28},{28,0},{1,5},{5... | collective-permute-start | bytes 172040 | tf_op jit(solution)/shard_map/ppermute | solution.py:47
  432.3 47.4 %collective-permute-start.1 = (bf16[2,32,448]{1,2,0:T(8,128)(2,1)}, bf16[2,32,448]{1,2,0:T(8,128)(2,1)S(1)}, u32[]{:S(2)}, u32[]{:S(2)}) collective-permute-start(bf16[2,32,448]{1,2,0:T(8,128)(2,1)} %get-tuple-element.19), channel_id=1, source_target_pairs={{0,28},{4,0},{8,4},{12,8},{16,12},{20,16},{24,20},{28,24},{1,29},{... | collective-permute-start | bytes 172040 | tf_op jit(solution)/shard_map/ppermute | solution.py:50
  441.9 37.8 %collective-permute-start.2 = (bf16[2,32,448]{1,2,0:T(8,128)(2,1)S(1)}, bf16[2,32,448]{1,2,0:T(8,128)(2,1)}, u32[]{:S(2)}, u32[]{:S(2)}) collective-permute-start(bf16[2,32,448]{1,2,0:T(8,128)(2,1)S(1)} %collective-permute-done), channel_id=1, source_target_pairs={{0,4},{4,8},{8,12},{12,16},{16,20},{20,24},{24,28},{28,0},{1,5},{5... | collective-permute-start | bytes 172040 | tf_op jit(solution)/shard_map/ppermute | solution.py:47
  444.4 37.3 %copy-start.8 = (f32[5,448]{1,0:T(8,128)S(1)}, f32[5,448]{1,0:T(8,128)}, u32[]{:S(2)}) copy-start(f32[5,448]{1,0:T(8,128)} %param.18) | copy-start | bytes 26884
  444.4 37.3 %copy-start.9 = (f32[5,448]{1,0:T(8,128)S(1)}, f32[5,448]{1,0:T(8,128)}, u32[]{:S(2)}) copy-start(f32[5,448]{1,0:T(8,128)} %param.17) | copy-start | bytes 26884
  479.7 9.6 %collective-permute-start.3 = (bf16[2,32,448]{1,2,0:T(8,128)(2,1)S(1)}, bf16[2,32,448]{1,2,0:T(8,128)(2,1)}, u32[]{:S(2)}, u32[]{:S(2)}) collective-permute-start(bf16[2,32,448]{1,2,0:T(8,128)(2,1)S(1)} %collective-permute-done.1), channel_id=1, source_target_pairs={{0,28},{4,0},{8,4},{12,8},{16,12},{20,16},{24,20},{28,24},{1,29},{... | collective-permute-start | bytes 172040 | tf_op jit(solution)/shard_map/ppermute | solution.py:50
  479.7 9.6 %collective-permute-start.4 = (bf16[2,32,448]{1,2,0:T(8,128)(2,1)}, bf16[2,32,448]{1,2,0:T(8,128)(2,1)}, u32[]{:S(2)}, u32[]{:S(2)}) collective-permute-start(bf16[2,32,448]{1,2,0:T(8,128)(2,1)} %collective-permute-done.2), channel_id=1, source_target_pairs={{0,4},{4,8},{8,12},{12,16},{16,20},{20,24},{24,28},{28,0},{1,5},{5... | collective-permute-start | bytes 172040 | tf_op jit(solution)/shard_map/ppermute | solution.py:47
  489.3 16.5 %collective-permute-start.5 = (bf16[2,32,448]{1,2,0:T(8,128)(2,1)}, bf16[2,32,448]{1,2,0:T(8,128)(2,1)}, u32[]{:S(2)}, u32[]{:S(2)}) collective-permute-start(bf16[2,32,448]{1,2,0:T(8,128)(2,1)} %collective-permute-done.3), channel_id=1, source_target_pairs={{0,28},{4,0},{8,4},{12,8},{16,12},{20,16},{24,20},{28,24},{1,29},{... | collective-permute-start | bytes 172040 | tf_op jit(solution)/shard_map/ppermute | solution.py:50
  489.3 19.0 %collective-permute-start.6 = (bf16[2,32,448]{1,2,0:T(8,128)(2,1)}, bf16[2,32,448]{1,2,0:T(8,128)(2,1)}, u32[]{:S(2)}, u32[]{:S(2)}) collective-permute-start(bf16[2,32,448]{1,2,0:T(8,128)(2,1)} %collective-permute-done.4), channel_id=1, source_target_pairs={{0,4},{4,8},{8,12},{12,16},{16,20},{20,24},{24,28},{28,0},{1,5},{5... | collective-permute-start | bytes 172040 | tf_op jit(solution)/shard_map/ppermute | solution.py:47
  510.0 0.8 copy-start.5
Sparse Core Ops, SparseCore 0:
  14.2 120.2 all-reduce.4
  149.6 70.4 all-reduce.6
  227.1 116.7 all-reduce.8
  358.2 70.4 all-reduce.10
